TPU v7x, 32 devices: a whole 2x2x4 slice. The times are simulated.
32 devices in a mesh: ctx: 16 (over z, x, core), head: 2 (over y).
Axes of the slice: x: 2, y: 2, z: 4, core: 2. Of those that a mesh axis runs over, the one named last changes fastest.
Arguments:
- queries: bfloat16 [16384, 1024], P(('ctx', 'head'))
- keys: bfloat16 [16384, 256], P(('ctx', 'head'))
- values: bfloat16 [16384, 256], P(('ctx', 'head')), may hold values from -6 to 6
- q_feature: bfloat16 [8, 128, 64], P('head'), may hold values from -0.5 to 0.5
- k_feature: bfloat16 [2, 128, 64], P('head'), may hold values from -0.5 to 0.5
- doc_lengths: int32 [64], replicated, may hold values from 1 to 7680, as said below
Outputs:
- attended: bfloat16 [16384, 1024], P('ctx', 'head')
Inputs may be any that keep to these rules, and one draw needn't show every extreme that they name: `doc_lengths`: positive lengths that sum to 16384; the first document has length 7680 and the second 3 * 1024.
All inputs are finite; a program needn't handle non-finite values.
Results may differ from a plain program's by a relative error of at most 0.0052.
Values may be sent and summed in bfloat16 or wider, within the bound.
A program may use at most 64 MiB of HBM per device.

v0:
```python
import jax
import jax.numpy as jnp
from jax import lax
from jax.sharding import PartitionSpec as P


def entering(x, axis, join, neutral):
    place = lax.axis_index(axis)
    gathered = jax.tree.map(
        lambda a, kind: lax.all_gather(a.astype(kind), axis),
        x,
        (jnp.bfloat16, jnp.bfloat16, jnp.bfloat16),
    )
    state = jax.tree.map(lambda a, e: jnp.zeros_like(a) + jnp.asarray(e, a.dtype), x, neutral)

    def one(turn, state):
        return join(
            state,
            jax.tree.map(
                lambda a, own: lax.dynamic_index_in_dim(a, turn, 0, False).astype(own.dtype),
                gathered,
                x,
            ),
        )

    return lax.fori_loop(0, place, one, state)


def hedgehog(inputs, weight):
    projected = jnp.einsum("nhd,hdf->nhf", inputs, weight, preferred_element_type=jnp.float32)
    return jnp.concatenate(
        [jax.nn.softmax(projected, -1), jax.nn.softmax(-projected, -1)], -1
    ).astype(jnp.bfloat16)


def doc_of(starts, positions):
    return jnp.sum((starts[None, :] <= positions[:, None]).astype(jnp.int32), 1) - 1


def combine_states(earlier, later):
    keep = 1.0 - later[2]
    return (
        later[0] + keep * earlier[0],
        later[1] + keep * earlier[1],
        jnp.maximum(earlier[2], later[2]),
    )


def body(queries, keys, values, q_feature, k_feature, doc_lengths):
    head_size = q_feature.shape[1]
    local_q, local_k, local_values = (
        lax.all_to_all(queries, "head", split_axis=1, concat_axis=0, tiled=True),
        lax.all_to_all(keys, "head", split_axis=1, concat_axis=0, tiled=True),
        lax.all_to_all(values, "head", split_axis=1, concat_axis=0, tiled=True),
    )
    length = local_q.shape[0]
    phi_q = hedgehog(local_q.reshape(length, -1, head_size), q_feature)
    phi_k = hedgehog(local_k.reshape(length, -1, head_size), k_feature)[:, 0, :]
    starts = jnp.cumsum(doc_lengths) - doc_lengths
    my_index = lax.axis_index("ctx")
    begin = my_index * length
    positions = begin + jnp.arange(length)
    doc_ids = doc_of(starts, positions)
    prev_doc = jnp.sum((starts <= begin - 1).astype(jnp.int32)) - 1
    last_mask = (doc_ids == doc_ids[-1]).astype(jnp.bfloat16)[:, None]
    chosen = phi_k * last_mask
    state_s = jnp.dot(chosen.T, local_values, preferred_element_type=jnp.float32)
    state_z = jnp.sum(chosen.astype(jnp.float32), 0)
    reset_flag = (doc_ids[-1] != prev_doc).astype(jnp.float32)
    identity = (jnp.zeros_like(state_s), jnp.zeros_like(state_z), jnp.zeros((), jnp.float32))
    carry_s, carry_z, unused_flag = entering(
        (state_s, state_z, reset_flag), "ctx", combine_states, identity
    )
    rows_index = jnp.arange(length)
    causal = (rows_index[None, :] <= rows_index[:, None]) & (doc_ids[:, None] == doc_ids[None, :])
    carried = (doc_ids == prev_doc).astype(jnp.float32)
    results = []
    for head_index in range(phi_q.shape[1]):
        phi_head = phi_q[:, head_index, :]
        scores = jnp.einsum("tf,sf->ts", phi_head, phi_k, preferred_element_type=jnp.float32)
        masked = jnp.where(causal, scores, 0.0)
        wide_head = phi_head.astype(jnp.float32)
        denominator = jnp.sum(masked, -1) + carried * jnp.dot(
            wide_head, carry_z, precision=lax.Precision.HIGHEST
        )
        numerator = jnp.dot(
            masked.astype(jnp.bfloat16), local_values, preferred_element_type=jnp.float32
        )
        numerator = numerator + carried[:, None] * jnp.dot(
            wide_head, carry_s, precision=lax.Precision.HIGHEST
        )
        results.append(numerator / denominator[:, None])
    return jnp.stack(results, 1).reshape(length, -1).astype(jnp.bfloat16)


def solution(mesh):
    placed = (
        P(("ctx", "head"), None),
        P(("ctx", "head"), None),
        P(("ctx", "head"), None),
        P("head", None, None),
        P("head", None, None),
        P(),
    )
    return jax.shard_map(
        body, mesh=mesh, in_specs=placed, out_specs=P("ctx", "head"), check_vma=False
    )
```

profile of v0, /device:TPU:31, one launch (start us, length us, event | category | flops | bytes accessed | tf_op | source)
XLA Modules:
  0.0 132.6 jit_solution(9762992069121839793)
XLA Ops:
  0.0 1.8 %copy.32 = bf16[512,256]{0,1:T(8,128)(2,1)} copy(bf16[512,256]{1,0:T(8,128)(2,1)} %param.9) | data formatting | bytes 524288 | tf_op args[1]
  1.8 3.7 %all-to-all-start.1 = ((bf16[512,2,128]{0,2,1:T(8,128)(2,1)}), bf16[512,2,128]{0,2,1:T(8,128)(2,1)S(1)}, u32[]{:S(2)}, u32[]{:S(2)}) async-start(bf16[512,2,128]{0,2,1:T(8,128)(2,1)} %bitcast.8), calls=%async_computation.1 | async-start | bytes 524288 | tf_op jit(solution)/shard_map/all_to_all | solution.py:53
  5.5 2.3 %copy.49 = bf16[64,2,8,512]{3,2,0,1:T(8,128)(2,1)} copy(bf16[64,2,8,512]{3,2,1,0:T(8,128)(2,1)} %bitcast.132) | data formatting | bytes 2097152 | tf_op jit(solution)/shard_map/all_to_all | solution.py:52
  7.8 0.7 copy.29
  8.5 0.1 reduce-window.9
  8.6 0.1 reduce.10
  8.7 1.4 %fusion.54 = (s32[]{:T(128)}, s32[64]{0:T(128)S(1)}) fusion(s32[]{:T(128)S(6)} %sub.64, s32[64]{0:T(128)S(1)} %reduce.10, s32[64]{0:T(128)} %param.13), kind=kLoop, calls=%fused_computation.97 | loop fusion | flops 255 | bytes 776 | tf_op jit(solution)/shard_map/reduce_sum | solution.py:64
  10.1 0.1 convert_reduce_fusion
  10.2 0.7 slice.17
  12.1 1.3 dynamic-slice
  13.4 0.7 dynamic-update-slice
  14.1 1.8 %copy.34 = bf16[512,256]{0,1:T(8,128)(2,1)} copy(bf16[512,256]{1,0:T(8,128)(2,1)} %param.10) | data formatting | bytes 524288 | tf_op args[2]
  15.9 29.0 %all-reduce = bf16[16]{0:T(256)(128)(2,1)S(1)} all-reduce(bf16[16]{0:T(256)(128)(2,1)S(1)} %dynamic-update-slice), channel_id=1, replica_groups=mesh['ctx'=16,'head'=2] {'ctx'}, use_global_device_ids=true, to_apply=%add | all-reduce | flops 16 | bytes 64
  44.9 0.6 compare_convert_fusion
  45.5 3.5 %all-to-all-start.2 = ((bf16[512,2,128]{0,2,1:T(8,128)(2,1)}), bf16[512,2,128]{0,2,1:T(8,128)(2,1)S(1)}, u32[]{:S(2)}, u32[]{:S(2)}) async-start(bf16[512,2,128]{0,2,1:T(8,128)(2,1)} %bitcast.16), calls=%async_computation.2 | async-start | bytes 524288 | tf_op jit(solution)/shard_map/all_to_all | solution.py:54
  49.0 0.2 copy.33
  49.2 0.2 fusion.73
  49.5 2.1 %all-to-all-done.2 = bf16[512,2,128]{0,2,1:T(8,128)(2,1)S(1)} async-done(((bf16[512,2,128]{0,2,1:T(8,128)(2,1)}), bf16[512,2,128]{0,2,1:T(8,128)(2,1)S(1)}, u32[]{:S(2)}, u32[]{:S(2)}) %all-to-all-start.2) | async-done | bytes 262176 | tf_op jit(solution)/shard_map/all_to_all | solution.py:54
  51.6 5.0 %all-to-all-start = ((bf16[512,2,512]{2,0,1:T(8,128)(2,1)}), bf16[512,2,512]{2,0,1:T(8,128)(2,1)S(1)}, u32[]{:S(2)}, u32[]{:S(2)}) async-start(bf16[512,2,512]{2,0,1:T(8,128)(2,1)} %bitcast.122), calls=%async_computation | async-start | bytes 2097152 | tf_op jit(solution)/shard_map/all_to_all | solution.py:52
  56.6 0.2 copy.35
  56.8 0.1 fusion.46
  56.9 0.1 fusion.51
  57.0 0.1 multiply_reduce_fusion
  57.2 0.2 convolution_convert_fusion
  57.4 23.0 %all-gather = bf16[2048,128]{1,0:T(8,128)(2,1)S(1)} all-gather(bf16[128,128]{1,0:T(8,128)(2,1)S(1)} %convolution_convert_fusion), channel_id=2, replica_groups=mesh['ctx'=16,'head'=2] {'ctx'}, dimensions={0}, use_global_device_ids=true | all-gather | bytes 557056 | tf_op jit(solution)/shard_map/all_gather | solution.py:10
  80.4 16.5 %all-gather.2 = bf16[16,1,128]{2,1,0:T(2,128)(2,1)S(1)} all-gather(bf16[1,1,128]{2,1,0:T(2,128)(2,1)S(1)} %bitcast.148), channel_id=3, replica_groups=mesh['ctx'=16,'head'=2] {'ctx'}, dimensions={0}, use_global_device_ids=true | all-gather | bytes 4352 | tf_op jit(solution)/shard_map/all_gather | solution.py:10
  97.0 20.2 %while.14 = (s32[]{:T(128)}, f32[128,128]{1,0:T(8,128)S(1)}, f32[128]{0:T(128)S(1)}, s32[]{:T(128)}, bf16[16,128,128]{2,1,0:T(8,128)(2,1)S(1)}, /*index=5*/bf16[...) while((s32[]{:T(128)}, f32[128,128]{1,0:T(8,128)S(1)}, ...), condition=%wide.region_13.14_spmd, body=%wide.region_12.13_spmd.sunk | while | flops 49542 | bytes 165297 | solution.py:26
  97.0 0.6 dynamic_slice.22
  98.3 0.6 dynamic_slice.22
  99.7 0.6 dynamic_slice.22
  101.0 0.6 dynamic_slice.22
  102.4 0.6 dynamic_slice.22
  103.7 0.6 dynamic_slice.22
  105.1 0.6 dynamic_slice.22
  106.4 0.6 dynamic_slice.22
  107.8 0.6 dynamic_slice.22
  109.1 0.6 dynamic_slice.22
  110.5 0.6 dynamic_slice.22
  111.8 0.6 dynamic_slice.22
  113.2 0.6 dynamic_slice.22
  114.5 0.6 dynamic_slice.22
  115.9 0.6 dynamic_slice.22
  117.2 0.3 reshape.120
  117.6 1.2 fusion.71
  118.7 1.2 fusion.72
  119.9 1.0 divide_convert_fusion
  121.0 0.8 fusion.69
  121.8 0.8 fusion.68
  122.5 0.2 fusion.59
  122.7 0.2 fusion.57
  123.0 0.8 fusion.67
  123.7 0.2 fusion.55
  123.9 0.2 fusion.61
  124.2 0.7 fusion.4
  124.9 0.7 fusion.5
  125.6 2.3 %select_reduce_fusion.3 = (f32[1024]{0:T(1024)S(1)}, f32[1024]{0:T(1024)S(1)}, f32[1024]{0:T(1024)S(1)}, f32[1024]{0:T(1024)S(1)}, bf16[1024,1024]{0,1:T(8,128)(2,1)S(1)}) fusion(s32[1024]{0:T(1024)S(1)} %broadcast_add_fusion, f32[1024,1024]{0,1:T(8,128)S(1)} %fusion.67, f32[1024,1024]{0,1:T(8,128)S(1)} %fusion.68, f32[1024,1024]{0,1:T(8,128)S(1)} %fusion.69, ...), kind=kOutput, calls=%fused_computation.12 | convolution fusion | flops 281538560 | bytes 15224832 | tf_op jit(solution)/shard_map/tf,sf->ts/dot_general | solution.py:80
  127.9 0.7 fusion.6
  128.6 0.7 fusion.3
  129.3 0.4 fusion.34
  129.8 0.4 fusion.33
  130.2 0.4 fusion.32
  130.7 0.4 fusion.31
  131.1 0.1 pad_maximum_fusion
  131.3 1.3 copy.36
  (51 shorter events, 0.7 us)
Async XLA Ops:
  0.0 117.5 %copy-start = (bf16[4,128,64]{1,2,0:T(8,128)(2,1)S(1)}, bf16[4,128,64]{1,2,0:T(8,128)(2,1)}, u32[]{:S(2)}) copy-start(bf16[4,128,64]{1,2,0:T(8,128)(2,1)} %param.11) | copy-start | bytes 196612
  0.0 49.2 %copy-start.3 = (bf16[1,128,64]{1,2,0:T(8,128)(2,1)S(1)}, bf16[1,128,64]{1,2,0:T(8,128)(2,1)}, u32[]{:S(2)}) copy-start(bf16[1,128,64]{1,2,0:T(8,128)(2,1)} %param.12) | copy-start | bytes 49156
  1.8 43.7 %all-to-all-start.1 = ((bf16[512,2,128]{0,2,1:T(8,128)(2,1)}), bf16[512,2,128]{0,2,1:T(8,128)(2,1)S(1)}, u32[]{:S(2)}, u32[]{:S(2)}) async-start(bf16[512,2,128]{0,2,1:T(8,128)(2,1)} %bitcast.8), calls=%async_computation.1 | async-start | bytes 524288 | tf_op jit(solution)/shard_map/all_to_all | solution.py:53
  45.5 6.0 %all-to-all-start.2 = ((bf16[512,2,128]{0,2,1:T(8,128)(2,1)}), bf16[512,2,128]{0,2,1:T(8,128)(2,1)S(1)}, u32[]{:S(2)}, u32[]{:S(2)}) async-start(bf16[512,2,128]{0,2,1:T(8,128)(2,1)} %bitcast.16), calls=%async_computation.2 | async-start | bytes 524288 | tf_op jit(solution)/shard_map/all_to_all | solution.py:54
  51.6 65.6 %all-to-all-start = ((bf16[512,2,512]{2,0,1:T(8,128)(2,1)}), bf16[512,2,512]{2,0,1:T(8,128)(2,1)S(1)}, u32[]{:S(2)}, u32[]{:S(2)}) async-start(bf16[512,2,512]{2,0,1:T(8,128)(2,1)} %bitcast.122), calls=%async_computation | async-start | bytes 2097152 | tf_op jit(solution)/shard_map/all_to_all | solution.py:52
  56.8 60.7 %copy-start.1 = (bf16[2,512,128]{2,1,0:T(8,128)(2,1)}, bf16[2,512,128]{2,1,0:T(8,128)(2,1)S(1)}, u32[]{:S(2)}) copy-start(bf16[2,512,128]{2,1,0:T(8,128)(2,1)S(1)} %copy.35) | copy-start | bytes 786436
  123.0 1.2 copy-start.2
where the time goes:
time: 133 us
  blocking collectives  68.5 us (52%)
  local copies, waits for them, and re-layouts  21 us (16%)
  matrix products  12.8 us (10%)
  starting transfers between devices  12.2 us (9%)
  loops' own time  9.98 us (8%)
  other arithmetic  4.46 us (3%)
  waiting for transfers between devices  2.14 us (2%)
  between operations  1.56 us (1%)
    all_gather x2, blocking collectives, entering(): lax.all_gather(a.astype(kind), axis)  39.6 us
    unnamed x1, blocking collectives  29 us
    another operation x1, loops' own time, entering(): return lax.fori_loop(0, place, one, state)  9.98 us
    dynamic_slice x15, local copies, waits for them, and re-layouts, one(): lax.dynamic_index_in_dim(a, turn, 0, False).astype(own.dtype)  9.73 us
    unnamed x14, local copies, waits for them, and re-layouts  5.66 us
    all_to_all x1, starting transfers between devices, body(): lax.all_to_all(queries, 'head', split_axis=1, concat_axis=0, tiled=True)  5.03 us
    dot_general x4, matrix products, body(): jnp.einsum('tf,sf->ts', phi_head, phi_k, preferred_element_type=jnp.float32)  4.59 us
    all_to_all x1, starting transfers between devices, body(): lax.all_to_all(keys, 'head', split_axis=1, concat_axis=0, tiled=True)  3.66 us
  transfers between devices with their start and end apart: 3, of which 1 were waited for; matrix products, arithmetic and copies ran while one was open for 16% of the time, Pallas kernels for 0%

commit v1 on v0

v1 whole, which is shorter than its diff:
```python
import functools

import jax
import jax.numpy as jnp
from jax import lax
from jax.experimental import pallas as pl
from jax.experimental.pallas import tpu as pltpu
from jax.sharding import PartitionSpec as P

MESH = pl.DeviceIdType.MESH
F32 = jnp.float32
BF16 = jnp.bfloat16
NT = (((1,), (1,)), ((), ()))
TN = (((0,), (0,)), ((), ()))
SECOND = 3 * 1024
ZROWS = 16


def iota(shape, dim):
    return lax.broadcasted_iota(jnp.int32, shape, dim)


def feature_map(x, w_ext, pair_sum):
    p = jnp.dot(x, w_ext, preferred_element_type=F32)
    first = iota(p.shape, 1) < p.shape[1] // 2
    top = jnp.max(jnp.where(first, p, -jnp.inf), 1, keepdims=True)
    low = jnp.max(jnp.where(first, -jnp.inf, p), 1, keepdims=True)
    e = jnp.exp(p - jnp.where(first, top, low))
    hi = e.astype(BF16)
    lo = (e - hi.astype(F32)).astype(BF16)
    total = jnp.dot(jnp.concatenate([hi, lo], 1), pair_sum, preferred_element_type=F32)
    return (e / total).astype(BF16)


def kernel(
    n_ctx, n_head, chunk, n0, n1, reach,
    q_hbm, k_hbm, v_hbm, wq_ref, wk_ref, len_ref, out_hbm,
    q_buf, k_buf, v_buf, phi_k, carry, state_out, state_in, out_buf,
    own_sem, kv_send, kv_recv, q_send, q_recv, s_send, s_recv, out_sem,
):
    me, b = lax.axis_index("head"), lax.axis_index("ctx")
    rows = q_hbm.shape[0]
    heads, length, hd = q_buf.shape
    per = rows // chunk
    chunks = length // chunk
    begin = b * length

    def last_of(j):
        return jnp.where(j < n0, n0 - 1, jnp.where(j < n1, n1 - 1, n_ctx - 1))

    def first_of(j):
        return jnp.where(j < n0, 0, jnp.where(j < n1, n0, n1))

    n_to = jnp.minimum(last_of(b) + 1, n_ctx - 1) - b
    n_from = jnp.where(b == 0, 0, b - first_of(b - 1))

    own = pl.ds(pl.multiple_of(me * rows, rows), rows)
    own_cols = pl.ds(pl.multiple_of(me * hd, hd), hd)
    own_copies = [
        pltpu.make_async_copy(k_hbm.at[:, own_cols], k_buf.at[own, :], own_sem.at[0]),
        pltpu.make_async_copy(v_hbm.at[:, own_cols], v_buf.at[own, :], own_sem.at[1]),
    ]
    for h in range(heads):
        cols = pl.ds(pl.multiple_of((me * heads + h) * hd, hd), hd)
        own_copies.append(
            pltpu.make_async_copy(q_hbm.at[:, cols], q_buf.at[h, own, :], own_sem.at[2 + h])
        )
    for c in own_copies:
        c.start()

    barrier = pltpu.get_barrier_semaphore()
    for o in range(1, n_head):
        pl.semaphore_signal(
            barrier, inc=1, device_id=(b, lax.rem(me + o, n_head)), device_id_type=MESH
        )

    def greet(i, _):
        @pl.when(i <= n_to)
        def _():
            pl.semaphore_signal(barrier, inc=1, device_id=(b + i, me), device_id_type=MESH)

        @pl.when(i <= n_from)
        def _():
            pl.semaphore_signal(barrier, inc=1, device_id=(b - i, me), device_id_type=MESH)

        return 0

    lax.fori_loop(1, reach + 1, greet, 0)

    docs = len_ref.shape[1]
    lens = jnp.broadcast_to(len_ref[...].astype(F32), (docs, docs))
    e_i, d_i = iota((docs, docs), 0), iota((docs, docs), 1)
    starts_col = jnp.sum(jnp.where(d_i < e_i, lens, 0.0), 1, keepdims=True)
    starts = jnp.sum(jnp.where(e_i == d_i, starts_col, 0.0), 0, keepdims=True)

    def doc_start(pos):
        return jnp.max(jnp.where(starts <= pos, starts, -1.0), 1, keepdims=True)

    lanes = 2 * hd
    half = hd // 2
    r_i, c_i = lax.rem(iota((lanes, hd), 0), hd), iota((lanes, hd), 1)
    pair_sum = ((r_i < half) == (c_i < half)).astype(F32).astype(BF16)
    ones = jnp.ones((chunk, hd), BF16)

    def widened(w):
        w = w.astype(F32)
        return jnp.concatenate([w, -w], 1).astype(BF16)

    wk = widened(wk_ref[0])
    wq = [widened(wq_ref[h]) for h in range(heads)]

    pl.semaphore_wait(barrier, n_head - 1 + n_to + n_from)

    def kv_copy(o, which):
        to = lax.rem(me + o, n_head)
        cols = pl.ds(pl.multiple_of(to * hd, hd), hd)
        src, dst = ((k_hbm, k_buf), (v_hbm, v_buf))[which]
        return pltpu.make_async_remote_copy(
            src_ref=src.at[:, cols],
            dst_ref=dst.at[own, :],
            send_sem=kv_send.at[o - 1, which],
            recv_sem=kv_recv.at[o - 1, which],
            device_id=(b, to),
            device_id_type=MESH,
        )

    def q_copy(o, i, h):
        to = lax.rem(me + o, n_head)
        cols = pl.ds(pl.multiple_of((to * heads + h) * hd, hd), hd)
        return pltpu.make_async_remote_copy(
            src_ref=q_hbm.at[pl.ds(i * chunk, chunk), cols],
            dst_ref=q_buf.at[h, pl.ds(pl.multiple_of(me * rows + i * chunk, chunk), chunk), :],
            send_sem=q_send.at[o - 1, i, h],
            recv_sem=q_recv.at[o - 1, i, h],
            device_id=(b, to),
            device_id_type=MESH,
        )

    for o in range(1, n_head):
        kv_copy(o, 0).start()
        kv_copy(o, 1).start()
    for o in range(1, n_head):
        for i in range(per):
            for h in range(heads):
                q_copy(o, i, h).start()

    def chunk_rows(c):
        return pl.ds(pl.multiple_of(c * chunk, chunk), chunk)

    def map_keys(c, _):
        phi_k[chunk_rows(c), :] = feature_map(k_buf[chunk_rows(c), :], wk, pair_sum)
        return 0

    def map_queries(c, _):
        for h in range(heads):
            q_buf[h, chunk_rows(c), :] = feature_map(q_buf[h, chunk_rows(c), :], wq[h], pair_sum)
        return 0

    for c in own_copies:
        c.wait()
    lax.fori_loop(me * per, me * per + per, map_keys, 0)
    lax.fori_loop(me * per, me * per + per, map_queries, 0)
    for o in range(1, n_head):
        kv_copy(o, 0).wait_recv()
        kv_copy(o, 1).wait_recv()
        peer = lax.rem(me - o + n_head, n_head)
        lax.fori_loop(peer * per, peer * per + per, map_keys, 0)

    total = jnp.zeros((2 * hd, hd), F32)
    for c in range(chunks):
        carry[c] = total
        c0 = begin + c * chunk
        edge = doc_start((c0 + chunk - 1).astype(F32))
        pos = (c0 + iota((chunk, 1), 0)).astype(F32)
        keys = phi_k[pl.ds(c * chunk, chunk), :]
        chosen = jnp.where(pos >= edge, keys.astype(F32), 0.0).astype(BF16)
        v_ext = jnp.concatenate([v_buf[pl.ds(c * chunk, chunk), :], ones], 1)
        new = lax.dot_general(v_ext, chosen, TN, preferred_element_type=F32)
        total = new + jnp.where(edge < c0.astype(F32), total, 0.0)
    state_out[...] = total[: hd + ZROWS].astype(BF16)

    def s_copy(i):
        return pltpu.make_async_remote_copy(
            src_ref=state_out,
            dst_ref=state_in.at[i - 1],
            send_sem=s_send.at[i - 1],
            recv_sem=s_recv.at[i - 1],
            device_id=(b + i, me),
            device_id_type=MESH,
        )

    def push(i, _):
        @pl.when(i <= n_to)
        def _():
            s_copy(i).start()

        return 0

    lax.fori_loop(1, reach + 1, push, 0)

    before = doc_start((begin - 1).astype(F32))
    state_sum = carry.at[chunks, pl.ds(0, hd + ZROWS), :]
    state_sum[...] = jnp.zeros((hd + ZROWS, hd), F32)

    def collect(i, _):
        @pl.when(i <= n_from)
        def _():
            s_copy(i).wait_recv()
            end = ((b - i + 1) * length - 1).astype(F32)
            state_sum[...] += jnp.where(end >= before, state_in[i - 1].astype(F32), 0.0)

        return 0

    lax.fori_loop(1, reach + 1, collect, 0)
    entering = state_sum[...]
    z_row = entering[hd : hd + 1]
    entering = jnp.concatenate([entering[:hd], jnp.broadcast_to(z_row, (hd, hd))], 0)

    def out_copy(c, h):
        return pltpu.make_async_copy(
            out_buf.at[h, chunk_rows(c), :],
            out_hbm.at[chunk_rows(c), pl.ds(h * hd, hd)],
            out_sem.at[c, h],
        )

    def attend(c, o=None, i=None):
        here = chunk_rows(c)
        c0 = begin + c * chunk
        pos = (c0 + iota((chunk, 1), 0)).astype(F32)
        lo = doc_start(pos)
        s_pos = (c0 + iota((chunk, chunk), 1)).astype(F32)
        mask = (s_pos <= pos) & (s_pos >= lo)
        carried = lo < c0.astype(F32)
        edge = doc_start((c0 - 1).astype(F32))
        held = carry[c] + jnp.where(edge < begin.astype(F32), entering, 0.0)
        held = held.astype(BF16)
        keys = phi_k[here, :]
        v_ext = jnp.concatenate([v_buf[here, :], ones], 1)
        for h in range(heads):
            if o is not None:
                q_copy(o, i, h).wait_recv()
                phi = feature_map(q_buf[h, here, :], wq[h], pair_sum)
            else:
                phi = q_buf[h, here, :]
            scores = lax.dot_general(phi, keys, NT, preferred_element_type=F32)
            weights = jnp.where(mask, scores, 0.0).astype(BF16)
            old = jnp.where(carried, phi.astype(F32), 0.0).astype(BF16)
            acc = jnp.dot(weights, v_ext, preferred_element_type=F32)
            acc += lax.dot_general(old, held, NT, preferred_element_type=F32)
            out_buf[h, here, :] = (acc[:, :hd] / acc[:, hd:]).astype(BF16)
            out_copy(c, h).start()

    def own_chunk(i, _):
        attend(me * per + i)
        return 0

    lax.fori_loop(0, per, own_chunk, 0)
    for o in range(1, n_head):
        peer = lax.rem(me - o + n_head, n_head)

        def peer_chunk(i, _):
            attend(peer * per + i, o, i)
            return 0

        lax.fori_loop(0, per, peer_chunk, 0)

    for o in range(1, n_head):
        kv_copy(o, 0).wait_send()
        kv_copy(o, 1).wait_send()
        for i in range(per):
            for h in range(heads):
                q_copy(o, i, h).wait_send()

    def pushed(i, _):
        @pl.when(i <= n_to)
        def _():
            s_copy(i).wait_send()

        return 0

    lax.fori_loop(1, reach + 1, pushed, 0)
    for c in range(chunks):
        for h in range(heads):
            out_copy(c, h).wait()


def body(n_ctx, n_head, queries, keys, values, q_feature, k_feature, doc_lengths):
    rows = queries.shape[0]
    heads, hd, _ = q_feature.shape
    length = rows * n_head
    tokens = length * n_ctx
    chunk = min(256, rows)
    chunks = length // chunk
    per = rows // chunk
    first = tokens // 2 - length // 2
    n0, n1 = first // length, (first + SECOND) // length
    reach = min(max(n0, n1 - n0, n_ctx - n1), n_ctx - 1)
    any_space = pl.BlockSpec(memory_space=pl.ANY)
    vmem = pl.BlockSpec(memory_space=pltpu.VMEM)
    dma = pltpu.SemaphoreType.DMA
    others = max(n_head - 1, 1)
    return pl.pallas_call(
        functools.partial(kernel, n_ctx, n_head, chunk, n0, n1, reach),
        out_shape=jax.ShapeDtypeStruct((length, heads * hd), BF16),
        in_specs=[any_space] * 3 + [vmem] * 3,
        out_specs=any_space,
        scratch_shapes=[
            pltpu.VMEM((heads, length, hd), BF16),
            pltpu.VMEM((length, hd), BF16),
            pltpu.VMEM((length, hd), BF16),
            pltpu.VMEM((length, hd), BF16),
            pltpu.VMEM((chunks + 1, 2 * hd, hd), F32),
            pltpu.VMEM((hd + ZROWS, hd), BF16),
            pltpu.VMEM((reach, hd + ZROWS, hd), BF16),
            pltpu.VMEM((heads, length, hd), BF16),
            dma((2 + heads,)),
            dma((others, 2)),
            dma((others, 2)),
            dma((others, per, heads)),
            dma((others, per, heads)),
            dma((reach,)),
            dma((reach,)),
            dma((chunks, heads)),
        ],
        compiler_params=pltpu.CompilerParams(
            collective_id=0, has_side_effects=True, vmem_limit_bytes=32 << 20
        ),
    )(queries, keys, values, q_feature, k_feature, doc_lengths.reshape(1, -1))


def solution(mesh):
    placed = (
        P(("ctx", "head"), None),
        P(("ctx", "head"), None),
        P(("ctx", "head"), None),
        P("head", None, None),
        P("head", None, None),
        P(),
    )
    return jax.shard_map(
        functools.partial(body, mesh.shape["ctx"], mesh.shape["head"]),
        mesh=mesh,
        in_specs=placed,
        out_specs=P("ctx", "head"),
        check_vma=False,
    )
```

time: 133 us -> 32 us (0.24)
  the two profiles are of different devices: /device:TPU:31 before, /device:TPU:11 now
where the time goes in v1:
time: 32 us; the launch traced here: 31.7 us
  Pallas kernels  25.8 us (81%)
  local copies, waits for them, and re-layouts  5.89 us (18%)
    pallas_call x1, Pallas kernels, body(): pl.pallas_call(functools.partial(kernel, n_ctx, n_head, chunk, n0, n1, re...  25.8 us
    unnamed x11, local copies, waits for them, and re-layouts  5.89 us

profile of v1, /device:TPU:11, one launch (start us, length us, event | category | flops | bytes accessed | tf_op | source)
XLA Modules:
  0.0 31.7 jit_solution(410431641076643961)
XLA Ops:
  0.0 0.8 %copy.8.wk_ref = bf16[1,128,64]{2,1,0:T(8,128)(2,1)S(1)} copy(bf16[1,128,64]{1,2,0:T(8,128)(2,1)} %param.10) | data formatting | bytes 32768 | tf_op args[4]
  0.8 0.0 copy-start.3
  0.8 1.0 %copy.7.wq_ref = bf16[4,128,64]{2,1,0:T(8,128)(2,1)S(1)} copy(bf16[4,128,64]{1,2,0:T(8,128)(2,1)} %param.9) | data formatting | bytes 131072 | tf_op args[3]
  1.8 0.0 copy-done.3
  1.8 0.0 copy-start
  1.8 1.2 %copy-done = bf16[512,1024]{1,0:T(8,128)(2,1)S(1)} copy-done((bf16[512,1024]{1,0:T(8,128)(2,1)S(1)}, bf16[512,1024]{1,0:T(8,128)(2,1)}, u32[]{:S(2)}) %copy-start) | copy-done | bytes 1048600
  3.1 0.0 copy-start.1
  3.1 0.9 %copy-done.1 = bf16[512,256]{1,0:T(8,128)(2,1)S(1)} copy-done((bf16[512,256]{1,0:T(8,128)(2,1)S(1)}, bf16[512,256]{1,0:T(8,128)(2,1)}, u32[]{:S(2)}) %copy-start.1) | copy-done | bytes 262168
  4.0 0.0 copy-start.2
  4.0 0.9 %copy-done.2 = bf16[512,256]{1,0:T(8,128)(2,1)S(1)} copy-done((bf16[512,256]{1,0:T(8,128)(2,1)S(1)}, bf16[512,256]{1,0:T(8,128)(2,1)}, u32[]{:S(2)}) %copy-start.2) | copy-done | bytes 262168
  5.0 25.8 %shard_map.64 = bf16[1024,512]{1,0:T(8,128)(2,1)S(1)} custom-call(bf16[512,1024]{1,0:T(8,128)(2,1)S(1)} %copy-done, bf16[512,256]{1,0:T(8,128)(2,1)S(1)} %copy-done.1, bf16[512,256]{1,0:T(8,128)(2,1)S(1)} %copy-done.2, bf16[4,128,64]{2,1,0:T(8,128)(2,1)S(1)} %copy.7.wq_ref, bf16[1,128,64]{2,1,0:T(8,128)(2,1)S(1)} %copy.8.wk_ref, s32[1,64]{1,0:T(1,128)S(1)} %bitcast.1), custom_call_target="tpu_custom_call" | custom-call | tf_op jit(solution)/shard_map/pallas_call | solution.py:302
  30.8 1.0 %copy.10 = bf16[1024,512]{1,0:T(8,128)(2,1)} copy(bf16[1024,512]{1,0:T(8,128)(2,1)S(1)} %shard_map.64) | data formatting | bytes 2097152
Async XLA Ops:
  0.8 1.0 %copy-start.3 = (s32[64]{0:T(128)S(1)}, s32[64]{0:T(128)}, u32[]{:S(2)}) copy-start(s32[64]{0:T(128)} %param.11) | copy-start | bytes 772
  1.8 1.2 %copy-start = (bf16[512,1024]{1,0:T(8,128)(2,1)S(1)}, bf16[512,1024]{1,0:T(8,128)(2,1)}, u32[]{:S(2)}) copy-start(bf16[512,1024]{1,0:T(8,128)(2,1)} %q_hbm.1) | copy-start | bytes 3145732
  3.1 0.9 %copy-start.1 = (bf16[512,256]{1,0:T(8,128)(2,1)S(1)}, bf16[512,256]{1,0:T(8,128)(2,1)}, u32[]{:S(2)}) copy-start(bf16[512,256]{1,0:T(8,128)(2,1)} %k_hbm.1) | copy-start | bytes 786436
  4.0 0.9 %copy-start.2 = (bf16[512,256]{1,0:T(8,128)(2,1)S(1)}, bf16[512,256]{1,0:T(8,128)(2,1)}, u32[]{:S(2)}) copy-start(bf16[512,256]{1,0:T(8,128)(2,1)} %v_hbm.1) | copy-start | bytes 786436

commit v2 on v1

--- a/solution.py
+++ b/solution.py
@@ -21,7 +21,7 @@
 
 
 def feature_map(x, w_ext, pair_sum):
-    p = jnp.dot(x, w_ext, preferred_element_type=F32)
+    p = lax.dot_general(x, w_ext, NT, preferred_element_type=F32)
     first = iota(p.shape, 1) < p.shape[1] // 2
     top = jnp.max(jnp.where(first, p, -jnp.inf), 1, keepdims=True)
     low = jnp.max(jnp.where(first, -jnp.inf, p), 1, keepdims=True)
@@ -104,7 +104,7 @@
 
     def widened(w):
         w = w.astype(F32)
-        return jnp.concatenate([w, -w], 1).astype(BF16)
+        return jnp.concatenate([w, -w], 0).astype(BF16)
 
     wk = widened(wk_ref[0])
     wq = [widened(wq_ref[h]) for h in range(heads)]
@@ -295,15 +295,15 @@
     first = tokens // 2 - length // 2
     n0, n1 = first // length, (first + SECOND) // length
     reach = min(max(n0, n1 - n0, n_ctx - n1), n_ctx - 1)
-    any_space = pl.BlockSpec(memory_space=pl.ANY)
+    hbm = pl.BlockSpec(memory_space=pltpu.HBM)
     vmem = pl.BlockSpec(memory_space=pltpu.VMEM)
     dma = pltpu.SemaphoreType.DMA
     others = max(n_head - 1, 1)
     return pl.pallas_call(
         functools.partial(kernel, n_ctx, n_head, chunk, n0, n1, reach),
         out_shape=jax.ShapeDtypeStruct((length, heads * hd), BF16),
-        in_specs=[any_space] * 3 + [vmem] * 3,
-        out_specs=any_space,
+        in_specs=[hbm] * 3 + [vmem] * 3,
+        out_specs=hbm,
         scratch_shapes=[
             pltpu.VMEM((heads, length, hd), BF16),
             pltpu.VMEM((length, hd), BF16),
@@ -323,9 +323,9 @@
             dma((chunks, heads)),
         ],
         compiler_params=pltpu.CompilerParams(
-            collective_id=0, has_side_effects=True, vmem_limit_bytes=32 << 20
+            collective_id=0, has_side_effects=True, vmem_limit_bytes=60 << 20
         ),
-    )(queries, keys, values, q_feature, k_feature, doc_lengths.reshape(1, -1))
+    )(queries, keys, values, q_feature.transpose(0, 2, 1), k_feature.transpose(0, 2, 1), doc_lengths.reshape(1, -1))
 
 
 def solution(mesh):

time: 32 us -> 28.6 us (0.89)
  the two profiles are of different devices: /device:TPU:11 before, /device:TPU:0 now
where the time goes in v2:
time: 28.6 us; the launch traced here: 28.5 us
  Pallas kernels  26.2 us (92%)
  local copies, waits for them, and re-layouts  2.26 us (8%)
    pallas_call x1, Pallas kernels, body(): pl.pallas_call(functools.partial(kernel, n_ctx, n_head, chunk, n0, n1, re...  26.2 us
    unnamed x1, local copies, waits for them, and re-layouts  2.26 us

profile of v2, /device:TPU:0, one launch (start us, length us, event | category | flops | bytes accessed | tf_op | source)
XLA Modules:
  0.0 28.5 jit_solution(7588708481300434534)
XLA Ops:
  0.0 26.2 %shard_map.64 = bf16[1024,512]{1,0:T(8,128)(2,1)} custom-call(bf16[512,1024]{1,0:T(8,128)(2,1)} %q_hbm.1, bf16[512,256]{1,0:T(8,128)(2,1)} %k_hbm.1, bf16[512,256]{1,0:T(8,128)(2,1)} %v_hbm.1, bf16[4,64,128]{2,1,0:T(8,128)(2,1)} %bitcast.3, bf16[1,64,128]{2,1,0:T(8,128)(2,1)} %bitcast.4, s32[1,64]{1,0:T(1,128)} %bitcast.5), custom_call_target="tpu_custom_call" | custom-call | tf_op jit(solution)/shard_map/pallas_call | solution.py:302
  26.2 2.3 %copy.8 = bf16[1024,512]{1,0:T(8,128)(2,1)} copy(bf16[1024,512]{1,0:T(8,128)(2,1)} %shard_map.64) | data formatting | bytes 2097152

commit v3 on v2

--- a/solution.py
+++ b/solution.py
@@ -34,9 +34,10 @@
 
 def kernel(
     n_ctx, n_head, chunk, n0, n1, reach,
-    q_hbm, k_hbm, v_hbm, wq_ref, wk_ref, len_ref, out_hbm,
-    q_buf, k_buf, v_buf, phi_k, carry, state_out, state_in, out_buf,
-    own_sem, kv_send, kv_recv, q_send, q_recv, s_send, s_recv, out_sem,
+    q_hbm, k_hbm, v_hbm, wq_hbm, wk_hbm, len_hbm, out_ref,
+    q_buf, k_buf, v_buf, phi_k, carry, state_out, state_in,
+    wq_ref, wk_ref, len_ref,
+    small_sem, own_sem, kv_send, kv_recv, q_send, q_recv, s_send, s_recv,
 ):
     me, b = lax.axis_index("head"), lax.axis_index("ctx")
     rows = q_hbm.shape[0]
@@ -53,6 +54,15 @@
 
     n_to = jnp.minimum(last_of(b) + 1, n_ctx - 1) - b
     n_from = jnp.where(b == 0, 0, b - first_of(b - 1))
+
+    small = [
+        pltpu.make_async_copy(src, dst, small_sem.at[i])
+        for i, (src, dst) in enumerate(
+            ((len_hbm, len_ref), (wk_hbm, wk_ref), (wq_hbm, wq_ref))
+        )
+    ]
+    for c in small:
+        c.start()
 
     own = pl.ds(pl.multiple_of(me * rows, rows), rows)
     own_cols = pl.ds(pl.multiple_of(me * hd, hd), hd)
@@ -87,6 +97,8 @@
 
     lax.fori_loop(1, reach + 1, greet, 0)
 
+    for c in small:
+        c.wait()
     docs = len_ref.shape[1]
     lens = jnp.broadcast_to(len_ref[...].astype(F32), (docs, docs))
     e_i, d_i = iota((docs, docs), 0), iota((docs, docs), 1)
@@ -215,13 +227,6 @@
     entering = state_sum[...]
     z_row = entering[hd : hd + 1]
     entering = jnp.concatenate([entering[:hd], jnp.broadcast_to(z_row, (hd, hd))], 0)
-
-    def out_copy(c, h):
-        return pltpu.make_async_copy(
-            out_buf.at[h, chunk_rows(c), :],
-            out_hbm.at[chunk_rows(c), pl.ds(h * hd, hd)],
-            out_sem.at[c, h],
-        )
 
     def attend(c, o=None, i=None):
         here = chunk_rows(c)
@@ -247,8 +252,7 @@
             old = jnp.where(carried, phi.astype(F32), 0.0).astype(BF16)
             acc = jnp.dot(weights, v_ext, preferred_element_type=F32)
             acc += lax.dot_general(old, held, NT, preferred_element_type=F32)
-            out_buf[h, here, :] = (acc[:, :hd] / acc[:, hd:]).astype(BF16)
-            out_copy(c, h).start()
+            out_ref[here, h * hd : (h + 1) * hd] = (acc[:, :hd] / acc[:, hd:]).astype(BF16)
 
     def own_chunk(i, _):
         attend(me * per + i)
@@ -279,9 +283,6 @@
         return 0
 
     lax.fori_loop(1, reach + 1, pushed, 0)
-    for c in range(chunks):
-        for h in range(heads):
-            out_copy(c, h).wait()
 
 
 def body(n_ctx, n_head, queries, keys, values, q_feature, k_feature, doc_lengths):
@@ -299,11 +300,16 @@
     vmem = pl.BlockSpec(memory_space=pltpu.VMEM)
     dma = pltpu.SemaphoreType.DMA
     others = max(n_head - 1, 1)
+    operands = (
+        queries, keys, values,
+        q_feature.transpose(0, 2, 1), k_feature.transpose(0, 2, 1),
+        doc_lengths.reshape(1, -1),
+    )
     return pl.pallas_call(
         functools.partial(kernel, n_ctx, n_head, chunk, n0, n1, reach),
         out_shape=jax.ShapeDtypeStruct((length, heads * hd), BF16),
-        in_specs=[hbm] * 3 + [vmem] * 3,
-        out_specs=hbm,
+        in_specs=[hbm] * 6,
+        out_specs=vmem,
         scratch_shapes=[
             pltpu.VMEM((heads, length, hd), BF16),
             pltpu.VMEM((length, hd), BF16),
@@ -312,7 +318,10 @@
             pltpu.VMEM((chunks + 1, 2 * hd, hd), F32),
             pltpu.VMEM((hd + ZROWS, hd), BF16),
             pltpu.VMEM((reach, hd + ZROWS, hd), BF16),
-            pltpu.VMEM((heads, length, hd), BF16),
+            pltpu.VMEM((heads, hd // 2, hd), BF16),
+            pltpu.VMEM((1, hd // 2, hd), BF16),
+            pltpu.VMEM((1, doc_lengths.shape[0]), jnp.int32),
+            dma((3,)),
             dma((2 + heads,)),
             dma((others, 2)),
             dma((others, 2)),
@@ -320,12 +329,11 @@
             dma((others, per, heads)),
             dma((reach,)),
             dma((reach,)),
-            dma((chunks, heads)),
         ],
         compiler_params=pltpu.CompilerParams(
-            collective_id=0, has_side_effects=True, vmem_limit_bytes=60 << 20
+            collective_id=0, has_side_effects=True, vmem_limit_bytes=32 << 20
         ),
-    )(queries, keys, values, q_feature.transpose(0, 2, 1), k_feature.transpose(0, 2, 1), doc_lengths.reshape(1, -1))
+    )(*[pltpu.with_memory_space_constraint(a, pltpu.HBM) for a in operands])
 
 
 def solution(mesh):

time: 28.6 us -> 25.9 us (0.906)
  Pallas kernels: 26.2 us -> 24.7 us
  local copies, waits for them, and re-layouts: 2.26 us -> 0.97 us
    pallas_call x1, Pallas kernels: 26.2 us -> 24.7 us  [body(): pl.pallas_call(functools.partial(kernel, n_ctx, n_head, chunk, n0, n1, re...]
    unnamed x1, local copies, waits for them, and re-layouts: 2.26 us -> 0.97 us
where the time goes in v3:
time: 25.9 us; the launch traced here: 25.7 us
  Pallas kernels  24.7 us (95%)
  local copies, waits for them, and re-layouts  0.97 us (4%)
    pallas_call x1, Pallas kernels, body(): pl.pallas_call(functools.partial(kernel, n_ctx, n_head, chunk, n0, n1, re...  24.7 us
    unnamed x1, local copies, waits for them, and re-layouts  0.97 us

profile of v3, /device:TPU:0, one launch (start us, length us, event | category | flops | bytes accessed | tf_op | source)
XLA Modules:
  0.0 25.7 jit_solution(9277082225605039162)
XLA Ops:
  0.0 24.7 %shard_map.64 = bf16[1024,512]{1,0:T(8,128)(2,1)S(1)} custom-call(bf16[512,1024]{1,0:T(8,128)(2,1)} %q_hbm.1, bf16[512,256]{1,0:T(8,128)(2,1)} %k_hbm.1, bf16[512,256]{1,0:T(8,128)(2,1)} %v_hbm.1, bf16[4,64,128]{2,1,0:T(8,128)(2,1)} %bitcast.3, bf16[1,64,128]{2,1,0:T(8,128)(2,1)} %bitcast.4, s32[1,64]{1,0:T(1,128)} %bitcast.5), custom_call_target="tpu_custom_call" | custom-call | tf_op jit(solution)/shard_map/pallas_call | solution.py:308
  24.8 1.0 %copy.8 = bf16[1024,512]{1,0:T(8,128)(2,1)} copy(bf16[1024,512]{1,0:T(8,128)(2,1)S(1)} %shard_map.64) | data formatting | bytes 2097152

commit v4 on v3

--- a/solution.py
+++ b/solution.py
@@ -290,7 +290,7 @@
     heads, hd, _ = q_feature.shape
     length = rows * n_head
     tokens = length * n_ctx
-    chunk = min(256, rows)
+    chunk = min(512, rows)
     chunks = length // chunk
     per = rows // chunk
     first = tokens // 2 - length // 2

time: 25.9 us -> 26.1 us (level)
  Pallas kernels: 24.7 us -> 25 us
where the time goes in v4:
time: 26.1 us; the launch traced here: 26 us
  Pallas kernels  25 us (96%)
  local copies, waits for them, and re-layouts  0.97 us (4%)
    pallas_call x1, Pallas kernels, body(): pl.pallas_call(functools.partial(kernel, n_ctx, n_head, chunk, n0, n1, re...  25 us
    unnamed x1, local copies, waits for them, and re-layouts  0.97 us

profile of v4, /device:TPU:0, one launch (start us, length us, event | category | flops | bytes accessed | tf_op | source)
XLA Modules:
  0.0 26.0 jit_solution(9126015779991421132)
XLA Ops:
  0.0 25.0 %shard_map.64 = bf16[1024,512]{1,0:T(8,128)(2,1)S(1)} custom-call(bf16[512,1024]{1,0:T(8,128)(2,1)} %q_hbm.1, bf16[512,256]{1,0:T(8,128)(2,1)} %k_hbm.1, bf16[512,256]{1,0:T(8,128)(2,1)} %v_hbm.1, bf16[4,64,128]{2,1,0:T(8,128)(2,1)} %bitcast.3, bf16[1,64,128]{2,1,0:T(8,128)(2,1)} %bitcast.4, s32[1,64]{1,0:T(1,128)} %bitcast.5), custom_call_target="tpu_custom_call" | custom-call | tf_op jit(solution)/shard_map/pallas_call | solution.py:308
  25.0 1.0 %copy.8 = bf16[1024,512]{1,0:T(8,128)(2,1)} copy(bf16[1024,512]{1,0:T(8,128)(2,1)S(1)} %shard_map.64) | data formatting | bytes 2097152
